TPU v7x, 32 devices: a whole 2x2x4 slice. The times are simulated.
32 devices in a mesh: seq: 8 (over z, core), mlp: 4 (over y, x).
Axes of the slice: x: 2, y: 2, z: 4, core: 2. Of those that a mesh axis runs over, the one named last changes fastest.
Arguments:
- layer_input: bfloat16 [3072, 5120], P('seq')
- attention_gain: bfloat16 [5120], replicated, may hold values from 0.099609375 to 1.8984375
- feedforward_gain: bfloat16 [5120], replicated, may hold values from 0.099609375 to 1.8984375
- query_weight: bfloat16 [5120, 4096], P('seq', 'mlp'), may hold values from -0.078125 to 0.078125
- key_weight: bfloat16 [5120, 1024], P('seq'), may hold values from -0.078125 to 0.078125
- value_weight: bfloat16 [5120, 1024], P('seq'), may hold values from -0.078125 to 0.078125
- out_weight: bfloat16 [4096, 5120], P('mlp', 'seq'), may hold values from -0.09375 to 0.09375
- gate_weight: bfloat16 [5120, 6912], P('seq', 'mlp'), may hold values from -0.078125 to 0.078125
- up_weight: bfloat16 [5120, 6912], P('seq', 'mlp'), may hold values from -0.078125 to 0.078125
- down_weight: bfloat16 [6912, 5120], P('mlp', 'seq'), may hold values from -0.078125 to 0.078125
- query_bias: bfloat16 [4096], P('mlp'), may hold values from -5 to 5
- key_bias: bfloat16 [1024], replicated, may hold values from -250 to 250
- value_bias: bfloat16 [1024], replicated, may hold values from -5 to 5
- doc_lengths: int32 [4], replicated, may hold values from 1 to 1536, 3072 in all
- piece_order: int32 [16], replicated, may hold values from 0 to 15, each once
- cache_page: int32 [16], replicated, may hold values from 0 to 15, each once
Outputs:
- layer_output: bfloat16 [3072, 5120], P(('seq', 'mlp'))
- kv_cache: bfloat16 [3072, 2048], P('seq', 'mlp')
Inputs may be any that keep to these rules, and one draw needn't show every extreme that they name: `doc_lengths`: the lengths sum to 3072, the longest is exactly 1536. `piece_order`: each piece number appears once. `cache_page`: each page number appears once.
All inputs are finite; a program needn't handle non-finite values.
Results may differ from a plain program's by a relative error of at most 0.0096.
Values may be sent and summed in bfloat16 or wider, within the bound.
No kernel may reach another device: no remote copies, remote signals or barrier semaphores. Data moves between devices by JAX's collectives and lax.ppermute only.
A program may use at most 192 MiB of HBM per device.

v0:
```python
import math
import jax
import jax.numpy as jnp
from jax import lax
from jax.sharding import PartitionSpec as P

KVH = 8
HD = 128
PIECES_DEV = 2
rope_base = 1000000.0
norm_eps = 1e-06
far_below = -1e30


def rms_scale(values, gain_vec):
    mean_sq = jnp.mean(values * values, axis=-1, keepdims=True)
    return values * lax.rsqrt(mean_sq + norm_eps) * gain_vec.astype(jnp.float32)


def rope_tables(position, head_dim):
    half_dim = head_dim // 2
    inverse_freq = jnp.power(
        jnp.float32(rope_base), -2.0 * jnp.arange(half_dim, dtype=jnp.float32) / head_dim
    )
    angles = position.astype(jnp.float32)[:, None] * inverse_freq[None, :]
    return (jnp.cos(angles), jnp.sin(angles))


def rotate(values, cosine, sine_part, head_count):
    row_count = values.shape[0]
    halves = values.reshape(row_count, head_count, 2, -1)
    lower_half = halves[:, :, 0, :]
    upper_half = halves[:, :, 1, :]
    cos_wide = cosine[:, None, :]
    sin_wide = sine_part[:, None, :]
    new_lower = lower_half * cos_wide - upper_half * sin_wide
    new_upper = upper_half * cos_wide + lower_half * sin_wide
    return jnp.stack([new_lower, new_upper], axis=2).reshape(row_count, -1)


def lookup(small_table, indices):
    matches = indices[:, None] == jnp.arange(small_table.shape[0], dtype=jnp.int32)[None, :]
    return jnp.sum(jnp.where(matches, small_table[None, :], 0), axis=1)


def stream_segment(doc_lengths, piece_order, row_ids, piece_len):
    stream = lookup(piece_order, row_ids // piece_len) * piece_len + row_ids % piece_len
    doc_ends = jnp.cumsum(doc_lengths)
    segment = jnp.sum((stream[:, None] >= doc_ends[None, :]).astype(jnp.int32), axis=1)
    return (stream, segment)


def stream_layout(doc_lengths, piece_order, row_ids, piece_len):
    stream, segment = stream_segment(doc_lengths, piece_order, row_ids, piece_len)
    doc_ends = jnp.cumsum(doc_lengths)
    doc_first = lookup(doc_ends - doc_lengths, segment)
    return (stream, segment, stream - doc_first)


def shards(
    layer_input,
    attention_gain,
    feedforward_gain,
    query_weight,
    key_weight,
    value_weight,
    out_weight,
    gate_weight,
    up_weight,
    down_weight,
    query_bias,
    key_bias,
    value_bias,
    doc_lengths,
    piece_order,
    cache_page,
):
    mlp_count = lax.axis_size("mlp")
    seq_rank = lax.axis_index("seq")
    mlp_rank = lax.axis_index("mlp")
    row_count = layer_input.shape[0]
    piece_len = row_count // PIECES_DEV
    kv_cols = max(HD, KVH * HD // mlp_count)
    kv_first = mlp_rank * KVH // mlp_count * HD
    key_weight = lax.dynamic_slice_in_dim(key_weight, kv_first, kv_cols, 1)
    value_weight = lax.dynamic_slice_in_dim(value_weight, kv_first, kv_cols, 1)
    key_bias = lax.dynamic_slice_in_dim(key_bias, kv_first, kv_cols, 0)
    value_bias = lax.dynamic_slice_in_dim(value_bias, kv_first, kv_cols, 0)
    query_weight, key_weight, value_weight, out_weight, gate_weight, up_weight, down_weight = (
        lax.all_gather(query_weight, "seq", axis=0, tiled=True),
        lax.all_gather(key_weight, "seq", axis=0, tiled=True),
        lax.all_gather(value_weight, "seq", axis=0, tiled=True),
        lax.all_gather(out_weight, "seq", axis=1, tiled=True),
        lax.all_gather(gate_weight, "seq", axis=0, tiled=True),
        lax.all_gather(up_weight, "seq", axis=0, tiled=True),
        lax.all_gather(down_weight, "seq", axis=1, tiled=True),
    )
    row_ids = seq_rank * row_count + jnp.arange(row_count, dtype=jnp.int32)
    stream, segment, position = stream_layout(doc_lengths, piece_order, row_ids, piece_len)
    cosine, sine_part = rope_tables(position, HD)
    residual = layer_input.astype(jnp.float32)
    normed = rms_scale(residual, attention_gain).astype(jnp.bfloat16)
    query = jnp.dot(normed, query_weight, preferred_element_type=jnp.float32) + query_bias.astype(
        jnp.float32
    )
    key_full = jnp.dot(normed, key_weight, preferred_element_type=jnp.float32) + key_bias.astype(
        jnp.float32
    )
    value_full = jnp.dot(
        normed, value_weight, preferred_element_type=jnp.float32
    ) + value_bias.astype(jnp.float32)
    own_cols = KVH * HD // mlp_count
    kv_heads = key_full.shape[1] // HD
    query_heads = query.shape[1] // HD
    per_kv = query_heads // kv_heads
    query_rot = rotate(query, cosine, sine_part, query_heads).astype(jnp.bfloat16)
    key_rot = rotate(key_full, cosine, sine_part, kv_heads).astype(jnp.bfloat16)
    value_b = value_full.astype(jnp.bfloat16)
    cache_width = 2 * own_cols
    group_size = max(1, HD // own_cols)
    offset = mlp_rank % group_size * cache_width
    piece_total = piece_order.shape[0]
    pieces = jnp.arange(piece_total, dtype=jnp.int32)
    page_ids = seq_rank * PIECES_DEV + jnp.arange(PIECES_DEV, dtype=jnp.int32)
    stream_of_page = jnp.sum(
        jnp.where(cache_page[None, :] == page_ids[:, None], pieces[None, :], 0), axis=1
    )
    source_piece = jnp.sum(
        jnp.where(piece_order[None, :] == stream_of_page[:, None], pieces[None, :], 0), axis=1
    )
    source_rows = (
        source_piece[:, None] * piece_len + jnp.arange(piece_len, dtype=jnp.int32)[None, :]
    ).reshape(row_count)
    query_grouped = query_rot.reshape(row_count, kv_heads, per_kv, HD)
    key_rows = lax.all_gather(key_rot, "seq", axis=0, tiled=True)
    value_rows = lax.all_gather(value_b, "seq", axis=0, tiled=True)
    row_top = jnp.full((kv_heads, per_kv, row_count), far_below, jnp.float32)
    cache_rows = jnp.zeros((row_count, cache_width), jnp.bfloat16)
    key_count = key_rows.shape[0]
    key_ids = jnp.arange(key_count, dtype=jnp.int32)
    key_stream, key_segment = stream_segment(doc_lengths, piece_order, key_ids, piece_len)
    allowed = (segment[:, None] == key_segment[None, :]) & (key_stream[None, :] <= stream[:, None])
    old_top = row_top
    scores = jnp.einsum(
        "qgrd,kgd->grqk",
        query_grouped,
        key_rows.reshape(key_count, kv_heads, HD),
        preferred_element_type=jnp.float32,
    ) / math.sqrt(HD)
    masked = jnp.where(allowed[None, None], scores, far_below)
    new_top = jnp.maximum(old_top, jnp.max(masked, axis=3))
    weights = jnp.where(allowed[None, None], jnp.exp(scores - new_top[..., None]), 0.0)
    new_total = jnp.sum(weights, axis=3)
    new_out = jnp.einsum(
        "grqk,kgd->grqd",
        weights.astype(jnp.bfloat16),
        value_rows.reshape(key_count, kv_heads, HD),
        preferred_element_type=jnp.float32,
    )
    row_top = new_top
    row_total = new_total
    partial_out = new_out
    inside = (source_rows >= 0) & (source_rows < key_count)
    cache_key_count = key_rows.shape[0]
    joined = jnp.stack(
        [
            key_rows.reshape(cache_key_count, kv_heads, HD),
            value_rows.reshape(cache_key_count, kv_heads, HD),
        ],
        axis=2,
    ).reshape(cache_key_count, 2 * kv_heads * HD)
    picked = jnp.take(
        lax.dynamic_slice_in_dim(joined, offset, cache_width, 1),
        jnp.clip(source_rows, 0, key_count - 1),
        axis=0,
    )
    cache_rows = jnp.where(inside[:, None], picked, cache_rows)
    row_top, row_total, partial_out, kv_cache = (row_top, row_total, partial_out, cache_rows)
    mixed = (
        (partial_out / row_total[..., None])
        .transpose(2, 0, 1, 3)
        .reshape(row_count, query_heads * HD)
        .astype(jnp.bfloat16)
    )
    attn_sum = lax.psum(
        jnp.dot(mixed, out_weight, preferred_element_type=jnp.float32).astype(jnp.bfloat16), "mlp"
    ).astype(jnp.float32)
    residual = residual + attn_sum
    normed2 = rms_scale(residual, feedforward_gain).astype(jnp.bfloat16)
    gate_act = jnp.dot(normed2, gate_weight, preferred_element_type=jnp.float32)
    up_act = jnp.dot(normed2, up_weight, preferred_element_type=jnp.float32)
    hidden_units = (jax.nn.silu(gate_act) * up_act).astype(jnp.bfloat16)
    share_rows = row_count // mlp_count
    down_sum = lax.psum_scatter(
        jnp.dot(hidden_units, down_weight, preferred_element_type=jnp.float32).astype(jnp.bfloat16),
        "mlp",
        scatter_dimension=0,
        tiled=True,
    ).astype(jnp.float32)
    own_residual = lax.dynamic_slice_in_dim(residual, mlp_rank * share_rows, share_rows, 0)
    layer_output = (own_residual + down_sum).astype(jnp.bfloat16)
    return (layer_output, kv_cache)


def solution(mesh):
    placed = (
        P("seq", None),
        P(),
        P(),
        P("seq", "mlp"),
        P("seq", None),
        P("seq", None),
        P("mlp", "seq"),
        P("seq", "mlp"),
        P("seq", "mlp"),
        P("mlp", "seq"),
        P("mlp"),
        P(),
        P(),
        P(),
        P(),
        P(),
    )
    return jax.shard_map(
        shards,
        mesh=mesh,
        in_specs=placed,
        out_specs=(P(("seq", "mlp"), None), P("seq", "mlp")),
        check_vma=False,
    )
```

profile of v0, /device:TPU:0, one launch (start us, length us, event | category | flops | bytes accessed | tf_op | source)
XLA Modules:
  0.0 1007.2 jit_solution(9585072494029778548)
XLA Ops:
  7.2 1.2 copy-done
  8.5 0.8 constant_dynamic-slice_fusion
  9.3 1.7 constant_dynamic-slice_fusion.1
  11.1 0.7 convert_element_type.79
  11.8 0.8 dynamic-slice_convert_fusion
  12.6 3.0 fusion.8
  15.6 31.3 %all-gather.16.cloned.1.call-done = bf16[5120,256]{1,0:T(8,128)(2,1)} async-done(((bf16[640,256]{1,0:T(8,128)(2,1)}), bf16[5120,256]{1,0:T(8,128)(2,1)}) %all-gather.16.cloned.1.call-update) | async-done | bytes 2621456 | tf_op jit(solution)/shard_map/all_gather | solution.py:92
  46.8 4.8 fusion.15
  51.8 0.5 all-gather.14.cloned.1.call-update
  52.4 0.2 reduce-window.8
  52.5 0.8 dynamic-slice_convert_fusion.1
  53.3 0.1 select_reduce_fusion.1
  53.4 0.1 convert_reduce_fusion.1
  53.5 0.1 select_reduce_fusion.2
  53.6 0.4 multiply_cosine_fusion
  54.1 27.3 %all-gather.10.cloned.1.call-done = bf16[5120,256]{1,0:T(8,128)(2,1)} async-done(((bf16[640,256]{1,0:T(8,128)(2,1)}), bf16[5120,256]{1,0:T(8,128)(2,1)}) %all-gather.10.cloned.1.call-update) | async-done | bytes 2621456 | tf_op jit(solution)/shard_map/all_gather | solution.py:91
  81.4 4.7 convolution_add_fusion.2
  86.1 0.1 subtract_convert_fusion.1
  86.2 0.7 pad_maximum_fusion.2
  87.0 0.5 all-gather.20.cloned.1.call-update
  87.5 0.2 all-reduce.2.cloned.1.call-start
  87.8 0.1 select_reduce_fusion
  87.9 0.1 convert_reduce_fusion
  88.0 2.2 compare_and_fusion
  90.2 18.1 %all-gather.18.cloned.1.call-done = bf16[3072,256]{1,0:T(8,128)(2,1)} async-done(((bf16[384,256]{1,0:T(8,128)(2,1)}), bf16[3072,256]{1,0:T(8,128)(2,1)}) %all-gather.18.cloned.1.call-update) | async-done | bytes 1572880 | tf_op jit(solution)/shard_map/all_gather | solution.py:136
  108.3 2.6 copy.45
  110.9 97.9 %all-gather.14.cloned.1.call-done = bf16[5120,1024]{1,0:T(8,128)(2,1)} async-done(((bf16[640,1024]{1,0:T(8,128)(2,1)}), bf16[5120,1024]{1,0:T(8,128)(2,1)}) %all-gather.14.cloned.1.call-update) | async-done | bytes 10485776 | tf_op jit(solution)/shard_map/all_gather | solution.py:90
  208.8 10.6 %convolution_add_fusion = f32[384,1024]{1,0:T(8,128)} fusion(bf16[5120,1024]{1,0:T(8,128)(2,1)} %all-gather.14.cloned.1.call-done, f32[1024]{0:T(1024)S(1)} %convert_element_type.84, bf16[384,5120]{1,0:T(8,128)(2,1)} %param.16, f32[5120]{0:T(1024)S(1)} %convert_element_type.79, f32[384]{0:T(512)S(1)} %add_rsqrt_fusion.1), kind=kOutput, calls=%fused_computation.27 | convolution fusion | flops 4034789376 | bytes 16016896 | tf_op jit(solution)/shard_map/dot_general | solution.py:103
  219.4 1.9 copy.32
  221.3 0.2 subtract_convert_fusion
  221.5 0.1 pad_maximum_fusion.1
  221.6 12.9 %all-gather.12.cloned.1.call-done = bf16[3072,256]{0,1:T(8,128)(2,1)} async-done(((bf16[384,256]{0,1:T(8,128)(2,1)}), bf16[3072,256]{0,1:T(8,128)(2,1)}) %all-gather.12.cloned.1.call-update) | async-done | bytes 1572880 | tf_op jit(solution)/shard_map/all_gather | solution.py:135
  234.4 17.0 %fusion = (f32[2,4,384]{2,1,0:T(4,128)S(1)}, f32[2,3072,384,4]{2,1,3,0:T(8,128)}) fusion(pred[384,3072]{0,1:T(8,128)(4,1)S(1)} %compare_and_fusion, bf16[3072,2,128,1]{0,2,3,1:T(8,128)(2,1)} %bitcast.52, bf16[384,2,4,128]{0,3,2,1:T(8,128)(2,1)S(1)} %bitcast.55), kind=kOutput, calls=%fused_computation.3 | convolution fusion | flops 2444227584 | bytes 41299968 | tf_op jit(solution)/shard_map/qgrd,kgd->grqk/dot_general | solution.py:144
  251.5 16.4 %fusion.3 = f32[2,4,384]{2,1,0:T(4,128)S(1)} fusion(f32[2,3072,384,4]{2,1,3,0:T(8,128)} %get-tuple-element.11, f32[2,4,384]{2,1,0:T(4,128)S(1)} %broadcast_maximum_fusion, pred[384,3072]{0,1:T(8,128)(4,1)S(1)} %compare_and_fusion), kind=kLoop, calls=%fused_computation.6 | loop fusion | flops 37745664 | bytes 38952960 | tf_op jit(solution)/shard_map/reduce_sum | solution.py:153
  267.9 15.9 %fusion.12 = bf16[384,2,4,128]{0,3,2,1:T(8,128)(2,1)} fusion(bf16[3072,2,128,1]{0,2,3,1:T(8,128)(2,1)S(1)} %bitcast.54, f32[2,3072,384,4]{2,1,3,0:T(8,128)} %get-tuple-element.11, f32[2,4,384]{2,1,0:T(4,128)S(1)} %broadcast_maximum_fusion, pred[384,3072]{0,1:T(8,128)(4,1)S(1)} %compare_and_fusion, f32[384,2,4]{0,2,1:T(4,128)S(1)} %bitcast.59), kind=kOutput, calls=%fused_computation.26 | convolution fusion | flops 2454454272 | bytes 41312256 | tf_op jit(solution)/shard_map/grqk,kgd->grqd/dot_general | solution.py:154
  283.8 50.7 %all-gather.20.cloned.1.call-done = bf16[1024,5120]{1,0:T(8,128)(2,1)} async-done(((bf16[1024,640]{1,0:T(8,128)(2,1)}), bf16[1024,5120]{1,0:T(8,128)(2,1)}) %all-gather.20.cloned.1.call-update) | async-done | bytes 10485776 | tf_op jit(solution)/shard_map/all_gather | solution.py:93
  334.5 10.5 %convolution_convert_fusion.1 = bf16[384,5120]{1,0:T(8,128)(2,1)} fusion(bf16[384,1024]{0,1:T(8,128)(2,1)} %bitcast.57, bf16[1024,5120]{1,0:T(8,128)(2,1)} %all-gather.20.cloned.1.call-done), kind=kOutput, calls=%fused_computation.19 | convolution fusion | flops 4028497920 | bytes 15204352 | tf_op jit(solution)/shard_map/dot_general | solution.py:186
  345.0 0.7 all-gather.22.cloned.1.call-update
  345.8 0.7 all-gather.24.cloned.1.call-update
  346.5 0.5 all-gather.26.cloned.1.call-update
  347.1 96.7 %all-reduce.2.cloned.1.call-done = bf16[384,5120]{1,0:T(8,128)(2,1)} async-done(((bf16[384,5120]{1,0:T(8,128)(2,1)}), bf16[384,5120]{1,0:T(8,128)(2,1)}) %all-reduce.2.cloned.1.call-update) | async-done | bytes 3932176 | tf_op jit(solution)/shard_map/psum | solution.py:185
  443.9 7.7 convert_add_fusion
  451.6 152.5 %all-gather.22.cloned.1.call-done = bf16[5120,1728]{0,1:T(8,128)(2,1)} async-done(((bf16[640,1728]{0,1:T(8,128)(2,1)}), bf16[5120,1728]{0,1:T(8,128)(2,1)}) %all-gather.22.cloned.1.call-update) | async-done | bytes 17694736 | tf_op jit(solution)/shard_map/all_gather | solution.py:94
  604.1 16.5 %fusion.36 = f32[384,1728]{0,1:T(8,128)} fusion(bf16[5120,1728]{0,1:T(8,128)(2,1)} %all-gather.22.cloned.1.call-done, f32[5120]{0:T(1024)S(1)} %convert_element_type.93, f32[384]{0:T(512)S(1)} %add_rsqrt_fusion, bf16[384,5120]{1,0:T(8,128)(2,1)} %param.16, bf16[384,5120]{1,0:T(8,128)(2,1)} %all-reduce.2.cloned.1.call-done), kind=kOutput, calls=%fused_computation.96 | convolution fusion | flops 6806568960 | bytes 28235264 | tf_op jit(solution)/shard_map/dot_general | solution.py:190
  620.6 142.0 %all-gather.24.cloned.1.call-done = bf16[5120,1728]{0,1:T(8,128)(2,1)} async-done(((bf16[640,1728]{0,1:T(8,128)(2,1)}), bf16[5120,1728]{0,1:T(8,128)(2,1)}) %all-gather.24.cloned.1.call-update) | async-done | bytes 17694736 | tf_op jit(solution)/shard_map/all_gather | solution.py:95
  762.6 158.3 %all-gather.26.cloned.1.call-done = bf16[1728,5120]{1,0:T(8,128)(2,1)} async-done(((bf16[1728,640]{1,0:T(8,128)(2,1)}), bf16[1728,5120]{1,0:T(8,128)(2,1)}) %all-gather.26.cloned.1.call-update) | async-done | bytes 17694736 | tf_op jit(solution)/shard_map/all_gather | solution.py:96
  921.0 27.9 %convolution_convert_fusion = bf16[384,5120]{1,0:T(8,128)(2,1)} fusion(bf16[1728,5120]{1,0:T(8,128)(2,1)} %all-gather.26.cloned.1.call-done, bf16[5120,1728]{0,1:T(8,128)(2,1)} %all-gather.24.cloned.1.call-done, f32[384,1728]{0,1:T(8,128)} %fusion.36, f32[5120]{0:T(1024)S(1)} %convert_element_type.93, f32[384]{0:T(512)S(1)} %add_rsqrt_fusion, ...), kind=kOutput, calls=%fused_computation.18 | convolution fusion | flops 13607288832 | bytes 49862144 | tf_op jit(solution)/shard_map/dot_general | solution.py:195
  948.9 0.6 copy-done.8
  949.5 0.2 fusion.32
  949.7 0.2 fusion.33
  949.9 0.1 fusion.25
  949.9 0.1 min.18
  950.0 0.1 min.16
  950.1 0.1 compare_and_fusion.1
  950.2 0.1 and.80
  950.3 5.0 copy.37
  955.4 1.9 stack_reshape.7
  957.2 6.4 pad_maximum_fusion
  963.6 13.4 %copy.38 = bf16[3072,2,2,128]{3,2,1,0:T(2,128)(2,1)} copy(bf16[3072,2,2,128]{3,1,0,2:T(2,128)(2,1)S(1)} %pad_maximum_fusion) | data formatting | bytes 6291456 | tf_op jit(solution)/shard_map/stack | solution.py:165
  977.0 5.8 reshape.328
  982.8 5.0 gather_fusion
  987.8 0.9 select_select_fusion
  988.7 9.0 reduce-scatter.2.cloned.1.call-done
  997.7 3.0 add_convert_fusion
  (49 shorter events, 0.7 us)
Async XLA Ops:
  7.2 1.3 copy-start
  7.2 39.7 %all-gather.16.cloned.1.call-start = ((), (), s32[]{:S(2)}) async-start(), calls=%async_computation.4 | async-start | bytes 2949120 | tf_op jit(solution)/shard_map/all_gather | solution.py:92
  9.3 72.1 %all-gather.10.cloned.1.call-start = ((), (), s32[]{:S(2)}) async-start(), calls=%async_computation.1 | async-start | bytes 2949120 | tf_op jit(solution)/shard_map/all_gather | solution.py:91
  11.1 97.2 %all-gather.18.cloned.1.call-start = ((), (), s32[]{:S(2)}) async-start(), calls=%async_computation.5 | async-start | bytes 1769472 | tf_op jit(solution)/shard_map/all_gather | solution.py:136
  15.6 36.8 %copy-start.7 = (s32[4]{0:T(128)S(1)}, s32[4]{0:T(128)}, u32[]{:S(2)}) copy-start(s32[4]{0:T(128)} %param.29) | copy-start | bytes 52
  15.6 37.7 %copy-start.6 = (s32[16]{0:T(128)S(1)}, s32[16]{0:T(128)}, u32[]{:S(2)}) copy-start(s32[16]{0:T(128)} %param.30) | copy-start | bytes 196
  51.7 157.1 %all-gather.14.cloned.1.call-start = ((), (), s32[]{:S(2)}) async-start(), calls=%async_computation.3 | async-start | bytes 11796480 | tf_op jit(solution)/shard_map/all_gather | solution.py:90
  52.3 182.2 %all-gather.12.cloned.1.call-start = ((), (), s32[]{:S(2)}) async-start(), calls=%async_computation.2 | async-start | bytes 1769472 | tf_op jit(solution)/shard_map/all_gather | solution.py:135
  54.1 33.7 %copy-start.5 = (bf16[1024]{0:T(1024)(128)(2,1)S(1)}, bf16[1024]{0:T(1024)(128)(2,1)}, u32[]{:S(2)}) copy-start(bf16[1024]{0:T(1024)(128)(2,1)} %param.26) | copy-start | bytes 6148
  86.9 247.6 %all-gather.20.cloned.1.call-start = ((), (), s32[]{:S(2)}) async-start(), calls=%async_computation.6 | async-start | bytes 11796480 | tf_op jit(solution)/shard_map/all_gather | solution.py:93
  87.5 356.4 %all-reduce.2.cloned.1.call-start = ((), (), s32[]{:S(2)}) async-start(), calls=%async_computation.7 | async-start | bytes 7864320 | tf_op jit(solution)/shard_map/psum | solution.py:185
  251.5 16.4 %copy-start.3 = (bf16[3072,256]{0,1:T(8,128)(2,1)S(1)}, bf16[3072,256]{0,1:T(8,128)(2,1)}, u32[]{:S(2)}) copy-start(bf16[3072,256]{0,1:T(8,128)(2,1)} %copy.45) | copy-start | bytes 4718596
  345.0 2.1 copy-start.4
  345.0 259.2 %all-gather.22.cloned.1.call-start = ((), (), s32[]{:S(2)}) async-start(), calls=%async_computation.8 | async-start | bytes 19906560 | tf_op jit(solution)/shard_map/all_gather | solution.py:94
  345.7 416.9 %all-gather.24.cloned.1.call-start = ((), (), s32[]{:S(2)}) async-start(), calls=%async_computation.9 | async-start | bytes 19906560 | tf_op jit(solution)/shard_map/all_gather | solution.py:95
  346.5 574.5 %all-gather.26.cloned.1.call-start = ((), (), s32[]{:S(2)}) async-start(), calls=%async_computation.10 | async-start | bytes 19906560 | tf_op jit(solution)/shard_map/all_gather | solution.py:96
  347.0 650.7 %reduce-scatter.2.cloned.1.call-start = ((), (), s32[]{:S(2)}) async-start(), calls=%async_computation.11 | async-start | bytes 4915200 | tf_op jit(solution)/shard_map/reduce_scatter | solution.py:194
  948.8 0.7 copy-start.8
  948.8 6.5 copy-start.2
  977.0 23.7 %copy-start.1 = (bf16[640,1024]{1,0:T(8,128)(2,1)S(1)}, bf16[640,1024]{1,0:T(8,128)(2,1)}, u32[]{:S(2)}) copy-start(bf16[640,1024]{1,0:T(8,128)(2,1)} %param.21) | copy-start | bytes 3932164
Sparse Core Ops, SparseCore 0:
  10.2 36.5 all-gather.15
  49.1 32.2 all-gather.9
  83.6 24.6 all-gather.17
  109.8 98.9 all-gather.13
  210.8 23.5 all-gather.11
  235.9 98.5 all-gather.19
  345.1 98.7 all-reduce.1
  445.6 158.5 all-gather.21
  605.8 156.7 all-gather.23
  764.2 156.7 all-gather.25
  949.0 48.7 reduce-scatter.1
where the time goes:
time: 1010 us
  waiting for transfers between devices  800 us (79%)
  matrix products  108 us (11%)
  other arithmetic  44.6 us (4%)
  local copies, waits for them, and re-layouts  40.1 us (4%)
  between operations  14.1 us (1%)
    all_gather x1, waiting for transfers between devices, shards(): lax.all_gather(down_weight, 'seq', axis=1, tiled=True)  158 us
    all_gather x1, waiting for transfers between devices, shards(): lax.all_gather(gate_weight, 'seq', axis=0, tiled=True)  153 us
    all_gather x1, waiting for transfers between devices, shards(): lax.all_gather(up_weight, 'seq', axis=0, tiled=True)  142 us
    all_gather x1, waiting for transfers between devices, shards(): lax.all_gather(query_weight, 'seq', axis=0, tiled=True)  97.9 us
    psum x1, waiting for transfers between devices, shards(): lax.psum(jnp.dot(mixed, out_weight, preferred_element_type=jnp.float32).a...  96.7 us
    all_gather x1, waiting for transfers between devices, shards(): lax.all_gather(out_weight, 'seq', axis=1, tiled=True)  50.7 us
    all_gather x1, waiting for transfers between devices, shards(): lax.all_gather(value_weight, 'seq', axis=0, tiled=True)  31.3 us
    dot_general x1, matrix products, shards(): jnp.dot(hidden_units, down_weight, preferred_element_type=jnp.float32)  27.9 us
  transfers between devices with their start and end apart: 11, of which 11 were waited for; matrix products, arithmetic and copies ran while one was open for 15% of the time, Pallas kernels for 0%

commit v1 on v0

--- a/solution.py
+++ b/solution.py
@@ -132,8 +132,11 @@
         source_piece[:, None] * piece_len + jnp.arange(piece_len, dtype=jnp.int32)[None, :]
     ).reshape(row_count)
     query_grouped = query_rot.reshape(row_count, kv_heads, per_kv, HD)
-    key_rows = lax.all_gather(key_rot, "seq", axis=0, tiled=True)
-    value_rows = lax.all_gather(value_b, "seq", axis=0, tiled=True)
+    key_rows, value_rows = jnp.split(
+        lax.all_gather(jnp.concatenate([key_rot, value_b], axis=1), "seq", axis=0, tiled=True),
+        [key_rot.shape[1]],
+        axis=1,
+    )
     row_top = jnp.full((kv_heads, per_kv, row_count), far_below, jnp.float32)
     cache_rows = jnp.zeros((row_count, cache_width), jnp.bfloat16)
     key_count = key_rows.shape[0]

time: 1010 us -> 998 us (0.988)
    reduce_scatter x1, waiting for transfers between devices: 9 us -> 24.1 us  [shards(): lax.psum_scatter(jnp.dot(hidden_units, down_weight, preferred_element_typ...]
    all_gather x1, waiting for transfers between devices: 50.7 us -> 37.4 us  [shards(): lax.all_gather(out_weight, 'seq', axis=1, tiled=True)]
    another operation x3 -> x1, local copies, waits for them, and re-layouts: 20.3 us -> 8.68 us  [shards(): jnp.stack([key_rows.reshape(cache_key_count, kv_heads, HD), value_rows.re...]
    all_gather x2 -> x1, waiting for transfers between devices: 31 us -> 33.5 us  [shards(): lax.all_gather(jnp.concatenate([key_rot, value_b], axis=1), 'seq', axis=0...]
  transfers between devices with their start and end apart: 11 -> 10, of which waited for: 11 -> 10; matrix products, arithmetic and copies ran while one was open for 15% -> 13% of each run, Pallas kernels for 0% -> 0%
where the time goes in v1:
time: 998 us; the launch traced here: 997 us
  waiting for transfers between devices  803 us (80%)
  matrix products  106 us (11%)
  other arithmetic  43 us (4%)
  local copies, waits for them, and re-layouts  30.3 us (3%)
  between operations  14.4 us (1%)
    all_gather x1, waiting for transfers between devices, shards(): lax.all_gather(down_weight, 'seq', axis=1, tiled=True)  158 us
    all_gather x1, waiting for transfers between devices, shards(): lax.all_gather(gate_weight, 'seq', axis=0, tiled=True)  153 us
    all_gather x1, waiting for transfers between devices, shards(): lax.all_gather(up_weight, 'seq', axis=0, tiled=True)  142 us
    psum x1, waiting for transfers between devices, shards(): lax.psum(jnp.dot(mixed, out_weight, preferred_element_type=jnp.float32).a...  96.6 us
    all_gather x1, waiting for transfers between devices, shards(): lax.all_gather(query_weight, 'seq', axis=0, tiled=True)  96.1 us
    all_gather x1, waiting for transfers between devices, shards(): lax.all_gather(out_weight, 'seq', axis=1, tiled=True)  37.4 us
    all_gather x1, waiting for transfers between devices, shards(): lax.all_gather(jnp.concatenate([key_rot, value_b], axis=1), 'seq', axis=0...  33.5 us
    all_gather x1, waiting for transfers between devices, shards(): lax.all_gather(value_weight, 'seq', axis=0, tiled=True)  30.3 us
  transfers between devices with their start and end apart: 10, of which 10 were waited for; matrix products, arithmetic and copies ran while one was open for 13% of the time, Pallas kernels for 0%

profile of v1, /device:TPU:0, one launch (start us, length us, event | category | flops | bytes accessed | tf_op | source)
XLA Modules:
  0.0 997.2 jit_solution(7562173861197720832)
XLA Ops:
  7.2 1.2 copy-done
  8.5 0.8 constant_dynamic-slice_fusion.1
  9.3 0.0 all-gather.11.cloned.1.call-start
  9.3 1.7 constant_dynamic-slice_fusion
  11.1 0.0 all-gather.13.cloned.1.call-start
  11.1 0.7 convert_element_type.79
  11.8 0.8 reduce-window.8
  12.7 0.8 dynamic-slice_convert_fusion
  13.5 0.7 select_reduce_fusion.1
  14.2 0.1 convert_reduce_fusion.1
  14.3 0.7 bitcast_subtract_fusion.1
  15.0 0.1 select_reduce_fusion.2
  15.1 3.0 fusion.8
  18.1 0.4 multiply_cosine_fusion
  18.5 28.4 %all-gather.9.cloned.1.call-done = bf16[5120,256]{1,0:T(8,128)(2,1)} async-done(((bf16[640,256]{1,0:T(8,128)(2,1)}), bf16[5120,256]{1,0:T(8,128)(2,1)}) %all-gather.9.cloned.1.call-update) | async-done | bytes 2621456 | tf_op jit(solution)/shard_map/all_gather | solution.py:91
  46.8 4.8 convolution_add_fusion.2
  51.6 0.1 subtract_convert_fusion.1
  51.7 30.3 %all-gather.11.cloned.1.call-done = bf16[5120,256]{1,0:T(8,128)(2,1)} async-done(((bf16[640,256]{1,0:T(8,128)(2,1)}), bf16[5120,256]{1,0:T(8,128)(2,1)}) %all-gather.11.cloned.1.call-update) | async-done | bytes 2621456 | tf_op jit(solution)/shard_map/all_gather | solution.py:92
  82.0 4.8 fusion.15
  86.7 0.8 pad_maximum_fusion.2
  87.6 0.5 all-gather.15.cloned.1.call-update
  88.2 0.5 all-gather.17.cloned.1.call-update
  88.7 0.2 all-reduce.2.cloned.1.call-start
  89.0 0.1 select_reduce_fusion
  89.1 0.1 convert_reduce_fusion
  89.2 2.2 compare_and_fusion
  91.4 33.5 %all-gather.13.cloned.1.call-done = bf16[3072,512]{0,1:T(8,128)(2,1)} async-done(((bf16[384,512]{0,1:T(8,128)(2,1)}), bf16[3072,512]{0,1:T(8,128)(2,1)}) %all-gather.13.cloned.1.call-update) | async-done | bytes 3145744 | tf_op jit(solution)/shard_map/all_gather | solution.py:136
  124.9 3.7 fusion.40
  128.7 96.1 %all-gather.15.cloned.1.call-done = bf16[5120,1024]{1,0:T(8,128)(2,1)} async-done(((bf16[640,1024]{1,0:T(8,128)(2,1)}), bf16[5120,1024]{1,0:T(8,128)(2,1)}) %all-gather.15.cloned.1.call-update) | async-done | bytes 10485776 | tf_op jit(solution)/shard_map/all_gather | solution.py:90
  224.8 10.6 %convolution_add_fusion = f32[384,1024]{1,0:T(8,128)} fusion(bf16[5120,1024]{1,0:T(8,128)(2,1)} %all-gather.15.cloned.1.call-done, f32[1024]{0:T(1024)S(1)} %convert_element_type.86, bf16[384,5120]{1,0:T(8,128)(2,1)} %param.16, f32[5120]{0:T(1024)S(1)} %convert_element_type.79, f32[384]{0:T(512)S(1)} %add_rsqrt_fusion.1), kind=kOutput, calls=%fused_computation.27 | convolution fusion | flops 4034789376 | bytes 16016896 | tf_op jit(solution)/shard_map/dot_general | solution.py:103
  235.4 1.9 copy.29
  237.3 0.2 subtract_convert_fusion
  237.6 0.1 pad_maximum_fusion.1
  237.7 1.1 copy-done.2
  238.7 15.5 %fusion = (f32[2,4,384]{2,1,0:T(4,128)S(1)}, f32[2,3072,384,4]{2,1,3,0:T(8,128)}) fusion(pred[384,3072]{0,1:T(8,128)(4,1)S(1)} %compare_and_fusion, bf16[3072,2,128,1]{0,2,3,1:T(8,128)(2,1)S(1)} %bitcast.53, bf16[384,2,4,128]{0,3,2,1:T(8,128)(2,1)S(1)} %bitcast.57), kind=kOutput, calls=%fused_computation.3 | convolution fusion | flops 2444227584 | bytes 41299968 | tf_op jit(solution)/shard_map/qgrd,kgd->grqk/dot_general | solution.py:147
  254.3 16.4 %fusion.3 = f32[2,4,384]{2,1,0:T(4,128)S(1)} fusion(f32[2,3072,384,4]{2,1,3,0:T(8,128)} %get-tuple-element.13, f32[2,4,384]{2,1,0:T(4,128)S(1)} %broadcast_maximum_fusion, pred[384,3072]{0,1:T(8,128)(4,1)S(1)} %compare_and_fusion), kind=kLoop, calls=%fused_computation.6 | loop fusion | flops 37745664 | bytes 38952960 | tf_op jit(solution)/shard_map/reduce_sum | solution.py:156
  270.7 15.9 %fusion.12 = bf16[384,2,4,128]{0,3,2,1:T(8,128)(2,1)} fusion(bf16[3072,2,128,1]{0,2,3,1:T(8,128)(2,1)S(1)} %bitcast.56, f32[2,3072,384,4]{2,1,3,0:T(8,128)} %get-tuple-element.13, f32[2,4,384]{2,1,0:T(4,128)S(1)} %broadcast_maximum_fusion, pred[384,3072]{0,1:T(8,128)(4,1)S(1)} %compare_and_fusion, f32[384,2,4]{0,2,1:T(4,128)S(1)} %bitcast.61), kind=kOutput, calls=%fused_computation.26 | convolution fusion | flops 2454454272 | bytes 41312256 | tf_op jit(solution)/shard_map/grqk,kgd->grqd/dot_general | solution.py:157
  286.6 37.4 %all-gather.17.cloned.1.call-done = bf16[1024,5120]{1,0:T(8,128)(2,1)} async-done(((bf16[1024,640]{1,0:T(8,128)(2,1)}), bf16[1024,5120]{1,0:T(8,128)(2,1)}) %all-gather.17.cloned.1.call-update) | async-done | bytes 10485776 | tf_op jit(solution)/shard_map/all_gather | solution.py:93
  324.0 10.4 %convolution_convert_fusion.1 = bf16[384,5120]{1,0:T(8,128)(2,1)} fusion(bf16[384,1024]{0,1:T(8,128)(2,1)} %bitcast.59, bf16[1024,5120]{1,0:T(8,128)(2,1)} %all-gather.17.cloned.1.call-done), kind=kOutput, calls=%fused_computation.19 | convolution fusion | flops 4028497920 | bytes 15204352 | tf_op jit(solution)/shard_map/dot_general | solution.py:189
  334.6 0.7 all-gather.19.cloned.1.call-update
  335.3 0.7 all-gather.21.cloned.1.call-update
  336.1 0.7 all-gather.23.cloned.1.call-update
  336.8 96.6 %all-reduce.2.cloned.1.call-done = bf16[384,5120]{1,0:T(8,128)(2,1)} async-done(((bf16[384,5120]{1,0:T(8,128)(2,1)}), bf16[384,5120]{1,0:T(8,128)(2,1)}) %all-reduce.2.cloned.1.call-update) | async-done | bytes 3932176 | tf_op jit(solution)/shard_map/psum | solution.py:188
  433.4 7.8 convert_add_fusion
  441.2 152.5 %all-gather.19.cloned.1.call-done = bf16[5120,1728]{0,1:T(8,128)(2,1)} async-done(((bf16[640,1728]{0,1:T(8,128)(2,1)}), bf16[5120,1728]{0,1:T(8,128)(2,1)}) %all-gather.19.cloned.1.call-update) | async-done | bytes 17694736 | tf_op jit(solution)/shard_map/all_gather | solution.py:94
  593.7 16.5 %fusion.36 = f32[384,1728]{0,1:T(8,128)} fusion(bf16[5120,1728]{0,1:T(8,128)(2,1)} %all-gather.19.cloned.1.call-done, f32[5120]{0:T(1024)S(1)} %convert_element_type.93, f32[384]{0:T(512)S(1)} %add_rsqrt_fusion, bf16[384,5120]{1,0:T(8,128)(2,1)} %param.16, bf16[384,5120]{1,0:T(8,128)(2,1)} %all-reduce.2.cloned.1.call-done), kind=kOutput, calls=%fused_computation.97 | convolution fusion | flops 6806568960 | bytes 28235264 | tf_op jit(solution)/shard_map/dot_general | solution.py:193
  610.2 142.0 %all-gather.21.cloned.1.call-done = bf16[5120,1728]{0,1:T(8,128)(2,1)} async-done(((bf16[640,1728]{0,1:T(8,128)(2,1)}), bf16[5120,1728]{0,1:T(8,128)(2,1)}) %all-gather.21.cloned.1.call-update) | async-done | bytes 17694736 | tf_op jit(solution)/shard_map/all_gather | solution.py:95
  752.2 158.5 %all-gather.23.cloned.1.call-done = bf16[1728,5120]{1,0:T(8,128)(2,1)} async-done(((bf16[1728,640]{1,0:T(8,128)(2,1)}), bf16[1728,5120]{1,0:T(8,128)(2,1)}) %all-gather.23.cloned.1.call-update) | async-done | bytes 17694736 | tf_op jit(solution)/shard_map/all_gather | solution.py:96
  910.6 27.9 %convolution_convert_fusion = bf16[384,5120]{1,0:T(8,128)(2,1)} fusion(bf16[1728,5120]{1,0:T(8,128)(2,1)} %all-gather.23.cloned.1.call-done, bf16[5120,1728]{0,1:T(8,128)(2,1)} %all-gather.21.cloned.1.call-done, f32[384,1728]{0,1:T(8,128)} %fusion.36, f32[5120]{0:T(1024)S(1)} %convert_element_type.93, f32[384]{0:T(512)S(1)} %add_rsqrt_fusion, ...), kind=kOutput, calls=%fused_computation.18 | convolution fusion | flops 13607288832 | bytes 49862144 | tf_op jit(solution)/shard_map/dot_general | solution.py:198
  938.6 0.6 copy-done.8
  939.2 0.2 fusion.32
  939.4 0.2 fusion.33
  939.5 0.1 fusion.25
  939.6 0.1 min.18
  939.7 0.1 min.16
  939.8 0.1 compare_and_fusion.1
  939.9 0.1 and.80
  940.0 3.4 pad_maximum_fusion
  943.4 8.7 copy.33
  952.1 5.9 reshape.328
  958.0 4.4 gather_fusion
  962.4 0.9 select_select_fusion
  963.3 24.1 %reduce-scatter.2.cloned.1.call-done = bf16[96,5120]{1,0:T(8,128)(2,1)} async-done(((bf16[384,5120]{1,0:T(8,128)(2,1)}), bf16[96,5120]{1,0:T(8,128)(2,1)}) %reduce-scatter.2.cloned.1.call-update) | async-done | bytes 983056 | tf_op jit(solution)/shard_map/reduce_scatter | solution.py:197
  987.4 3.0 add_convert_fusion
  (44 shorter events, 0.6 us)
Async XLA Ops:
  7.2 1.3 copy-start
  7.2 39.7 %all-gather.9.cloned.1.call-start = ((), (), s32[]{:S(2)}) async-start(), calls=%async_computation.1 | async-start | bytes 2949120 | tf_op jit(solution)/shard_map/all_gather | solution.py:91
  9.3 72.7 %all-gather.11.cloned.1.call-start = ((), (), s32[]{:S(2)}) async-start(), calls=%async_computation.2 | async-start | bytes 2949120 | tf_op jit(solution)/shard_map/all_gather | solution.py:92
  11.1 113.9 %all-gather.13.cloned.1.call-start = ((), (), s32[]{:S(2)}) async-start(), calls=%async_computation.3 | async-start | bytes 3538944 | tf_op jit(solution)/shard_map/all_gather | solution.py:136
  82.0 7.0 copy-start.6
  82.0 7.0 copy-start.7
  87.6 137.3 %all-gather.15.cloned.1.call-start = ((), (), s32[]{:S(2)}) async-start(), calls=%async_computation.4 | async-start | bytes 11796480 | tf_op jit(solution)/shard_map/all_gather | solution.py:90
  88.1 235.9 %all-gather.17.cloned.1.call-start = ((), (), s32[]{:S(2)}) async-start(), calls=%async_computation.5 | async-start | bytes 11796480 | tf_op jit(solution)/shard_map/all_gather | solution.py:93
  88.7 344.7 %all-reduce.2.cloned.1.call-start = ((), (), s32[]{:S(2)}) async-start(), calls=%async_computation.6 | async-start | bytes 7864320 | tf_op jit(solution)/shard_map/psum | solution.py:188
  237.3 1.4 copy-start.2
  254.3 16.4 %copy-start.4 = (bf16[3072,256]{0,1:T(8,128)(2,1)S(1)}, bf16[3072,256]{0,1:T(8,128)(2,1)}, u32[]{:S(2)}) copy-start(bf16[3072,256]{0,1:T(8,128)(2,1)} %get-tuple-element.5) | copy-start | bytes 4718596
  334.5 2.3 copy-start.5
  334.5 259.2 %all-gather.19.cloned.1.call-start = ((), (), s32[]{:S(2)}) async-start(), calls=%async_computation.7 | async-start | bytes 19906560 | tf_op jit(solution)/shard_map/all_gather | solution.py:94
  335.3 416.9 %all-gather.21.cloned.1.call-start = ((), (), s32[]{:S(2)}) async-start(), calls=%async_computation.8 | async-start | bytes 19906560 | tf_op jit(solution)/shard_map/all_gather | solution.py:95
  336.0 574.6 %all-gather.23.cloned.1.call-start = ((), (), s32[]{:S(2)}) async-start(), calls=%async_computation.9 | async-start | bytes 19906560 | tf_op jit(solution)/shard_map/all_gather | solution.py:96
  336.8 650.7 %reduce-scatter.2.cloned.1.call-start = ((), (), s32[]{:S(2)}) async-start(), calls=%async_computation.10 | async-start | bytes 4915200 | tf_op jit(solution)/shard_map/reduce_scatter | solution.py:197
  938.5 0.7 copy-start.8
  938.5 1.5 copy-start.3
  952.1 38.3 %copy-start.1 = (bf16[640,1024]{1,0:T(8,128)(2,1)S(1)}, bf16[640,1024]{1,0:T(8,128)(2,1)}, u32[]{:S(2)}) copy-start(bf16[640,1024]{1,0:T(8,128)(2,1)} %param.20) | copy-start | bytes 3932164
Sparse Core Ops, SparseCore 0:
  10.2 36.5 all-gather.8
  49.1 32.8 all-gather.10
  87.7 37.2 all-gather.12
  126.4 98.3 all-gather.14
  226.3 97.7 all-gather.16
  334.6 98.7 all-reduce.1
  435.1 158.5 all-gather.18
  595.4 156.7 all-gather.20
  753.9 156.7 all-gather.22
  938.7 48.7 reduce-scatter.1
